TPU v7x, 32 devices: a whole 2x2x4 slice. The times are simulated.
32 devices in a mesh: grp: 8 (over z, core), sp: 4 (over y, x).
Axes of the slice: x: 2, y: 2, z: 4, core: 2. Of those that a mesh axis runs over, the one named last changes fastest.
Arguments:
- acts: bfloat16 [32, 4, 16, 728], P('grp', 'sp'), may hold values from -6 to 6
- cotangent: bfloat16 [32, 4, 16, 728], P(('grp', 'sp')), may hold values from -6 to 6
- depth_kernel: float32 [3, 3, 728], replicated, may hold values from -2 to 2
- point_weight: bfloat16 [728, 728], replicated, may hold values from -0.21875 to 0.21875
- batch_norm_gain: float32 [728], replicated, may hold values from 0.5 to 2
- norm_shift_bias: float32 [728], replicated, may hold values from -1 to 1
Outputs:
- block_out: bfloat16 [32, 4, 16, 728], P(('grp', 'sp'))
- input_grad: bfloat16 [32, 4, 16, 728], P('grp', 'sp')
- weight_grad: float32 [529984], P('sp')
All inputs are finite; a program needn't handle non-finite values.
Results may differ from a plain program's by a relative error of at most 0.018.
Values may be sent and summed in bfloat16 or wider, within the bound.
A program may use at most 64 MiB of HBM per device.

v0:
```python
import jax
import jax.numpy as jnp
from jax import lax
from jax.sharding import PartitionSpec as P


def depth_forward(field, filter_weight):
    rows = field.shape[1]
    cols = field.shape[2]
    padded = jnp.pad(field, ((0, 0), (1, 1), (1, 1), (0, 0)))
    total = jnp.zeros(field.shape, jnp.float32)
    for i in range(3):
        for j in range(3):
            total = total + padded[:, i : i + rows, j : j + cols, :] * filter_weight[i, j]
    return total


def depth_backward(field, filter_weight):
    rows = field.shape[1]
    cols = field.shape[2]
    padded = jnp.pad(field, ((0, 0), (1, 1), (1, 1), (0, 0)))
    total = jnp.zeros(field.shape, jnp.float32)
    for i in range(3):
        for j in range(3):
            total = (
                total
                + padded[:, 2 - i : 2 - i + rows, 2 - j : 2 - j + cols, :] * filter_weight[i, j]
            )
    return total


def body(acts, cotangent, depth_kernel, point_weight, batch_norm_gain, norm_shift_bias):
    channel_count = acts.shape[-1]
    sample_image = lax.all_to_all(acts, "sp", split_axis=0, concat_axis=1, tiled=True)
    input_single_precision = sample_image.astype(jnp.float32)
    hidden = jnp.maximum(input_single_precision, 0.0)
    depthed = depth_forward(hidden, depth_kernel).astype(jnp.bfloat16)
    flat_d = depthed.reshape(-1, channel_count)
    element_count = flat_d.shape[0] * lax.axis_size("sp")
    projected_output = jnp.dot(flat_d, point_weight, preferred_element_type=jnp.float32)
    total, squares = lax.psum(
        (jnp.sum(projected_output, axis=0), jnp.sum(projected_output * projected_output, axis=0)),
        "sp",
    )
    batch_mean = total / element_count
    var = squares / element_count - batch_mean * batch_mean
    inverse_deviation = lax.rsqrt(var + 1e-05)
    normalized_input = (projected_output - batch_mean) * inverse_deviation
    block_out = (
        (
            input_single_precision.reshape(-1, channel_count)
            + batch_norm_gain * normalized_input
            + norm_shift_bias
        )
        .astype(jnp.bfloat16)
        .reshape(sample_image.shape)
    )
    gfloat = cotangent.astype(jnp.float32).reshape(-1, channel_count)
    scaled_output = gfloat * batch_norm_gain
    leading_layer, second_layer = lax.psum(
        (jnp.sum(scaled_output, axis=0), jnp.sum(scaled_output * normalized_input, axis=0)), "sp"
    )
    projected_gradient = (
        inverse_deviation
        * (
            scaled_output
            - leading_layer / element_count
            - normalized_input * (second_layer / element_count)
        )
    ).astype(jnp.bfloat16)
    local_weight = jnp.dot(
        flat_d.T, projected_gradient, preferred_element_type=jnp.float32
    ).reshape(-1)
    ddepth = jnp.dot(
        projected_gradient, point_weight.T, preferred_element_type=jnp.float32
    ).reshape(sample_image.shape)
    dhidden = depth_backward(ddepth, depth_kernel)
    dinput = (
        gfloat.reshape(sample_image.shape) + jnp.where(sample_image > 0, dhidden, 0.0)
    ).astype(jnp.bfloat16)
    input_grad = lax.all_to_all(dinput, "sp", split_axis=1, concat_axis=0, tiled=True)
    slices = lax.psum_scatter(
        local_weight.astype(jnp.bfloat16), "sp", scatter_dimension=0, tiled=True
    ).astype(jnp.float32)
    weight_grad = lax.psum(slices, "grp")
    return (block_out, input_grad, weight_grad)


def solution(mesh):
    in_specs = (P("grp", "sp", None, None), P(("grp", "sp"), None, None, None), P(), P(), P(), P())
    out_specs = (P(("grp", "sp"), None, None, None), P("grp", "sp", None, None), P("sp"))
    return jax.shard_map(body, mesh=mesh, in_specs=in_specs, out_specs=out_specs, check_vma=False)
```

profile of v0, /device:TPU:0, one launch (start us, length us, event | category | flops | bytes accessed | tf_op | source)
XLA Modules:
  0.0 160.6 jit_solution(10437990497592473162)
XLA Ops:
  7.2 5.3 %all-to-all-start = ((bf16[4,1,16,728]{3,2,1,0:T(8,128)(2,1)}), bf16[4,1,16,728]{3,2,1,0:T(8,128)(2,1)S(1)}, u32[]{:S(2)}, u32[]{:S(2)}) async-start(bf16[4,1,16,728]{3,2,1,0:T(8,128)(2,1)} %param.6), calls=%async_computation | async-start | bytes 196608 | tf_op jit(solution)/shard_map/all_to_all | solution.py:34
  12.5 0.0 all-reduce.10.cloned.1.call-start
  12.6 1.0 multiply_reduce_fusion.1
  13.5 1.0 slice_reduce_fusion.8
  14.5 3.0 %all-to-all-done = bf16[4,1,16,728]{3,2,1,0:T(8,128)(2,1)S(1)} async-done(((bf16[4,1,16,728]{3,2,1,0:T(8,128)(2,1)}), bf16[4,1,16,728]{3,2,1,0:T(8,128)(2,1)S(1)}, u32[]{:S(2)}, u32[]{:S(2)}) %all-to-all-start) | async-done | bytes 93216 | tf_op jit(solution)/shard_map/all_to_all | solution.py:34
  17.5 0.1 fusion.9
  17.6 0.3 fusion.39
  18.0 8.4 %all-reduce.4 = (f32[728]{0:T(1024)S(1)}, f32[728]{0:T(1024)S(1)}) all-reduce(f32[728]{0:T(1024)S(1)} %get-tuple-element.7, f32[728]{0:T(1024)S(1)} %get-tuple-element.6), channel_id=1, replica_groups=mesh['grp'=8,'sp'=4] {'sp'}, use_global_device_ids=true, to_apply=%region_3.4 | all-reduce | flops 1456 | bytes 11648 | tf_op jit(solution)/shard_map/psum | solution.py:41
  26.5 0.1 multiply_reduce_fusion
  26.5 9.0 %all-reduce.3 = (f32[728]{0:T(1024)S(1)}, f32[728]{0:T(1024)S(1)}) all-reduce(f32[728]{0:T(1024)S(1)} %multiply_reduce_fusion, f32[728]{0:T(1024)S(1)} %multiply_reduce_fusion.1), channel_id=1, replica_groups=mesh['grp'=8,'sp'=4] {'sp'}, use_global_device_ids=true, to_apply=%region_7.8 | all-reduce | flops 1456 | bytes 11648 | tf_op jit(solution)/shard_map/psum | solution.py:60
  35.6 0.7 multiply_convert_fusion
  36.3 0.5 convolution_convert_fusion
  36.8 3.5 %convert_element_type.59 = bf16[529984]{0:T(1024)(128)(2,1)} reshape(bf16[728,728]{1,0:T(8,128)(2,1)S(1)} %convolution_convert_fusion) | data formatting | bytes 2119936 | tf_op jit(solution)/shard_map/convert_element_type | solution.py:83
  40.3 0.0 all-reduce.10.cloned.1.call-update
  40.3 0.0 all-reduce.8.cloned.1.call-start
  40.3 0.6 dynamic-slice
  41.6 0.5 fusion.40
  42.1 51.5 %all-reduce.10.cloned.1.call-done = bf16[529984]{0:T(1024)(128)(2,1)} async-done(((bf16[529984]{0:T(1024)(128)(2,1)}), bf16[529984]{0:T(1024)(128)(2,1)}) %all-reduce.10.cloned.1.call-update) | async-done | bytes 1059984
  93.5 1.9 %dynamic-slice_convert_fusion = f32[132496]{0:T(1024)} fusion(bf16[529984]{0:T(1024)(128)(2,1)} %all-reduce.10.cloned.1.call-done, u32[]{:T(128)S(6)} %multiply.5), kind=kLoop, calls=%fused_computation.17 | loop fusion | flops 132496 | bytes 794980 | tf_op jit(solution)/shard_map/convert_element_type | solution.py:84
  95.5 0.2 fusion.38
  95.7 7.7 %all_to_all.21 = bf16[1,4,16,728]{3,2,0,1:T(8,128)(2,1)S(1)} all-to-all(bf16[1,4,16,728]{3,2,0,1:T(8,128)(2,1)S(1)} %fusion.38), channel_id=1, replica_groups=mesh['grp'=8,'sp'=4] {'sp'}, dimensions={1} | all-to-all | bytes 186368 | tf_op jit(solution)/shard_map/all_to_all | solution.py:81
  103.4 47.9 %all-reduce.8.cloned.1.call-done = f32[132496]{0:T(1024)} async-done(((f32[132496]{0:T(1024)}), f32[132496]{0:T(1024)}) %all-reduce.8.cloned.1.call-update) | async-done | bytes 530000 | tf_op jit(solution)/shard_map/psum | solution.py:85
  151.3 0.6 copy.16
  151.9 1.9 %copy.17 = f32[132496]{0:T(1024)} copy(f32[132496]{0:T(1024)} %all-reduce.8.cloned.1.call-done) | data formatting | bytes 1059968
  (15 shorter events, 0.1 us)
Async XLA Ops:
  7.2 10.5 %copy-start = (bf16[728,728]{1,0:T(8,128)(2,1)S(1)}, bf16[728,728]{1,0:T(8,128)(2,1)}, u32[]{:S(2)}) copy-start(bf16[728,728]{1,0:T(8,128)(2,1)} %param.9) | copy-start | bytes 3179908
  7.2 10.3 %all-to-all-start = ((bf16[4,1,16,728]{3,2,1,0:T(8,128)(2,1)}), bf16[4,1,16,728]{3,2,1,0:T(8,128)(2,1)S(1)}, u32[]{:S(2)}, u32[]{:S(2)}) async-start(bf16[4,1,16,728]{3,2,1,0:T(8,128)(2,1)} %param.6), calls=%async_computation | async-start | bytes 196608 | tf_op jit(solution)/shard_map/all_to_all | solution.py:34
  12.5 13.9 %copy-start.1 = (bf16[1,4,16,728]{3,2,1,0:T(8,128)(2,1)S(1)}, bf16[1,4,16,728]{3,2,1,0:T(8,128)(2,1)}, u32[]{:S(2)}) copy-start(bf16[1,4,16,728]{3,2,1,0:T(8,128)(2,1)} %param.7) | copy-start | bytes 279556
  12.5 13.9 %copy-start.2 = (f32[728]{0:T(1024)S(1)}, f32[728]{0:T(1024)}, u32[]{:S(2)}) copy-start(f32[728]{0:T(1024)} %param.10) | copy-start | bytes 8740
  12.5 81.0 %all-reduce.10.cloned.1.call-start = ((), (), s32[]{:S(2)}) async-start(), calls=%async_computation.3 | async-start | bytes 2121728
  17.6 18.0 %copy-start.3 = (f32[728]{0:T(1024)S(1)}, f32[728]{0:T(1024)}, u32[]{:S(2)}) copy-start(f32[728]{0:T(1024)} %param.11) | copy-start | bytes 8740
  36.8 3.5 %copy-start.4 = (u32[32]{0:T(128)S(1)}, u32[32]{0:T(128)}, u32[]{:S(2)}) copy-start(u32[32]{0:T(128)} %constant.23) | copy-start | bytes 388
  40.3 111.0 %all-reduce.8.cloned.1.call-start = ((), (), s32[]{:S(2)}) async-start(), calls=%async_computation.2 | async-start | bytes 1064960 | tf_op jit(solution)/shard_map/psum | solution.py:85
Sparse Core Ops, SparseCore 0:
  40.4 53.0 all-reduce.9
  96.5 54.7 all-reduce.7
where the time goes:
time: 161 us
  waiting for transfers between devices  102 us (63%)
  blocking collectives  25.1 us (16%)
  between operations  14.8 us (9%)
  local copies, waits for them, and re-layouts  7.53 us (5%)
  starting transfers between devices  5.41 us (3%)
  other arithmetic  4.04 us (3%)
    unnamed x3, waiting for transfers between devices  51.5 us
    psum x1, waiting for transfers between devices, body(): weight_grad = lax.psum(slices, 'grp')  47.9 us
    psum x1, blocking collectives, body(): lax.psum((jnp.sum(scaled_output, axis=0), jnp.sum(scaled_output * normali...  8.99 us
    psum x1, blocking collectives, body(): lax.psum((jnp.sum(projected_output, axis=0), jnp.sum(projected_output * p...  8.45 us
    all_to_all x1, blocking collectives, body(): lax.all_to_all(dinput, 'sp', split_axis=1, concat_axis=0, tiled=True)  7.68 us
    all_to_all x1, starting transfers between devices, body(): lax.all_to_all(acts, 'sp', split_axis=0, concat_axis=1, tiled=True)  5.34 us
    convert_element_type x1, local copies, waits for them, and re-layouts, body(): local_weight.astype(jnp.bfloat16)  3.46 us
  transfers between devices with their start and end apart: 3, of which 3 were waited for; matrix products, arithmetic and copies ran while one was open for 2% of the time, Pallas kernels for 0%

commit v1 on v0

--- a/solution.py
+++ b/solution.py
@@ -82,7 +82,7 @@
     slices = lax.psum_scatter(
         local_weight.astype(jnp.bfloat16), "sp", scatter_dimension=0, tiled=True
     ).astype(jnp.float32)
-    weight_grad = lax.psum(slices, "grp")
+    weight_grad = jnp.sum(lax.all_gather(slices, axis_name="grp"), 0)
     return (block_out, input_grad, weight_grad)
 
 

time: 161 us -> 217 us (1.35)
  waiting for transfers between devices: 102 us -> 143 us
  local copies, waits for them, and re-layouts: 7.53 us -> 14.9 us
  other arithmetic: 4.04 us -> 10.7 us
    unnamed x3 -> x4, waiting for transfers between devices: 51.5 us -> 140 us
    psum x1 -> x0, waiting for transfers between devices: 47.9 us -> none  [body(): weight_grad = lax.psum(slices, 'grp')]
    all_gather x0 -> x1, local copies, waits for them, and re-layouts: none -> 6.5 us  [body(): weight_grad = jnp.sum(lax.all_gather(slices, axis_name='grp'), 0)]
    reduce_sum x0 -> x1, other arithmetic: none -> 6.23 us  [body(): weight_grad = jnp.sum(lax.all_gather(slices, axis_name='grp'), 0)]
    unnamed x0 -> x1, other arithmetic: none -> 2.35 us
where the time goes in v1:
time: 217 us; the launch traced here: 216 us
  waiting for transfers between devices  143 us (66%)
  blocking collectives  25.1 us (12%)
  between operations  15.5 us (7%)
  local copies, waits for them, and re-layouts  14.9 us (7%)
  other arithmetic  10.7 us (5%)
  starting transfers between devices  5.41 us (2%)
    unnamed x4, waiting for transfers between devices  140 us
    psum x1, blocking collectives, body(): lax.psum((jnp.sum(scaled_output, axis=0), jnp.sum(scaled_output * normali...  8.99 us
    psum x1, blocking collectives, body(): lax.psum((jnp.sum(projected_output, axis=0), jnp.sum(projected_output * p...  8.45 us
    all_to_all x1, blocking collectives, body(): lax.all_to_all(dinput, 'sp', split_axis=1, concat_axis=0, tiled=True)  7.68 us
    all_gather x1, local copies, waits for them, and re-layouts, body(): weight_grad = jnp.sum(lax.all_gather(slices, axis_name='grp'), 0)  6.5 us
    reduce_sum x1, other arithmetic, body(): weight_grad = jnp.sum(lax.all_gather(slices, axis_name='grp'), 0)  6.23 us
    all_to_all x1, starting transfers between devices, body(): lax.all_to_all(acts, 'sp', split_axis=0, concat_axis=1, tiled=True)  5.34 us
  transfers between devices with their start and end apart: 3, of which 3 were waited for; matrix products, arithmetic and copies ran while one was open for 2% of the time, Pallas kernels for 0%

profile of v1, /device:TPU:0, one launch (start us, length us, event | category | flops | bytes accessed | tf_op | source)
XLA Modules:
  0.0 216.2 jit_solution(15554500893325686421)
XLA Ops:
  7.2 5.3 %all-to-all-start = ((bf16[4,1,16,728]{3,2,1,0:T(8,128)(2,1)}), bf16[4,1,16,728]{3,2,1,0:T(8,128)(2,1)S(1)}, u32[]{:S(2)}, u32[]{:S(2)}) async-start(bf16[4,1,16,728]{3,2,1,0:T(8,128)(2,1)} %param.6), calls=%async_computation | async-start | bytes 196608 | tf_op jit(solution)/shard_map/all_to_all | solution.py:34
  12.6 1.0 multiply_reduce_fusion.1
  13.5 0.9 slice_reduce_fusion.8
  14.5 3.0 %all-to-all-done = bf16[4,1,16,728]{3,2,1,0:T(8,128)(2,1)S(1)} async-done(((bf16[4,1,16,728]{3,2,1,0:T(8,128)(2,1)}), bf16[4,1,16,728]{3,2,1,0:T(8,128)(2,1)S(1)}, u32[]{:S(2)}, u32[]{:S(2)}) %all-to-all-start) | async-done | bytes 93216 | tf_op jit(solution)/shard_map/all_to_all | solution.py:34
  17.5 0.1 fusion.9
  17.6 0.3 fusion.39
  18.0 8.4 %all-reduce.5 = (f32[728]{0:T(1024)S(1)}, f32[728]{0:T(1024)S(1)}) all-reduce(f32[728]{0:T(1024)S(1)} %get-tuple-element.10, f32[728]{0:T(1024)S(1)} %get-tuple-element.9), channel_id=1, replica_groups=mesh['grp'=8,'sp'=4] {'sp'}, use_global_device_ids=true, to_apply=%region_3.4 | all-reduce | flops 1456 | bytes 11648 | tf_op jit(solution)/shard_map/psum | solution.py:41
  26.5 0.1 multiply_reduce_fusion
  26.5 9.0 %all-reduce.4 = (f32[728]{0:T(1024)S(1)}, f32[728]{0:T(1024)S(1)}) all-reduce(f32[728]{0:T(1024)S(1)} %multiply_reduce_fusion, f32[728]{0:T(1024)S(1)} %multiply_reduce_fusion.1), channel_id=1, replica_groups=mesh['grp'=8,'sp'=4] {'sp'}, use_global_device_ids=true, to_apply=%region_7.8 | all-reduce | flops 1456 | bytes 11648 | tf_op jit(solution)/shard_map/psum | solution.py:60
  35.6 0.7 multiply_convert_fusion
  36.3 0.5 convolution_convert_fusion
  36.8 3.5 %convert_element_type.57 = bf16[529984]{0:T(1024)(128)(2,1)} reshape(bf16[728,728]{1,0:T(8,128)(2,1)S(1)} %convolution_convert_fusion) | data formatting | bytes 2119936 | tf_op jit(solution)/shard_map/convert_element_type | solution.py:83
  40.4 0.6 dynamic-slice.1
  41.6 0.6 dynamic-slice
  42.8 50.7 %all-reduce.11.cloned.1.call-done = bf16[529984]{0:T(1024)(128)(2,1)} async-done(((bf16[529984]{0:T(1024)(128)(2,1)}), bf16[529984]{0:T(1024)(128)(2,1)}) %all-reduce.11.cloned.1.call-update) | async-done | bytes 1059984
  93.5 2.1 broadcast.72
  95.7 2.3 %convert_dynamic-update-slice_fusion = f32[1059968]{0:T(1024)} fusion(f32[1059968]{0:T(1024)} %broadcast.72, u32[]{:T(128)} %bitcast.11, bf16[529984]{0:T(1024)(128)(2,1)} %all-reduce.11.cloned.1.call-done, u32[]{:T(128)S(6)} %multiply.8), kind=kLoop, calls=%fused_computation.17 | loop fusion | flops 132496 | bytes 799236
  98.1 0.5 fusion.40
  98.5 0.2 fusion.38
  98.7 7.7 %all_to_all.21 = bf16[1,4,16,728]{3,2,0,1:T(8,128)(2,1)S(1)} all-to-all(bf16[1,4,16,728]{3,2,0,1:T(8,128)(2,1)S(1)} %fusion.38), channel_id=1, replica_groups=mesh['grp'=8,'sp'=4] {'sp'}, dimensions={1} | all-to-all | bytes 186368 | tf_op jit(solution)/shard_map/all_to_all | solution.py:81
  106.4 89.6 %all-reduce.9.cloned.1.call-done = f32[1059968]{0:T(1024)} async-done(((f32[1059968]{0:T(1024)}), f32[1059968]{0:T(1024)}) %all-reduce.9.cloned.1.call-update) | async-done | bytes 4239888
  196.0 6.5 %reshape.127 = f32[8,132496]{1,0:T(8,128)} reshape(f32[1059968]{0:T(1024)} %all-reduce.9.cloned.1.call-done) | data formatting | bytes 8479744 | tf_op jit(solution)/shard_map/all_gather | solution.py:85
  202.5 6.2 %reduce_sum.49 = f32[132496]{0:T(1024)} reduce(f32[8,132496]{1,0:T(8,128)} %reshape.127, f32[]{:T(128)} %constant.5.clone.1), dimensions={0}, to_apply=%region_9.10 | reduce | flops 927472 | bytes 4769860 | tf_op jit(solution)/shard_map/reduce_sum | solution.py:85
  208.7 0.6 copy.20
  (20 shorter events, 0.2 us)
Async XLA Ops:
  7.2 10.5 %copy-start = (bf16[728,728]{1,0:T(8,128)(2,1)S(1)}, bf16[728,728]{1,0:T(8,128)(2,1)}, u32[]{:S(2)}) copy-start(bf16[728,728]{1,0:T(8,128)(2,1)} %param.9) | copy-start | bytes 3179908
  7.2 10.3 %all-to-all-start = ((bf16[4,1,16,728]{3,2,1,0:T(8,128)(2,1)}), bf16[4,1,16,728]{3,2,1,0:T(8,128)(2,1)S(1)}, u32[]{:S(2)}, u32[]{:S(2)}) async-start(bf16[4,1,16,728]{3,2,1,0:T(8,128)(2,1)} %param.6), calls=%async_computation | async-start | bytes 196608 | tf_op jit(solution)/shard_map/all_to_all | solution.py:34
  12.5 13.9 %copy-start.1 = (bf16[1,4,16,728]{3,2,1,0:T(8,128)(2,1)S(1)}, bf16[1,4,16,728]{3,2,1,0:T(8,128)(2,1)}, u32[]{:S(2)}) copy-start(bf16[1,4,16,728]{3,2,1,0:T(8,128)(2,1)} %param.7) | copy-start | bytes 279556
  12.5 13.9 %copy-start.2 = (f32[728]{0:T(1024)S(1)}, f32[728]{0:T(1024)}, u32[]{:S(2)}) copy-start(f32[728]{0:T(1024)} %param.10) | copy-start | bytes 8740
  12.5 81.0 %all-reduce.11.cloned.1.call-start = ((), (), s32[]{:S(2)}) async-start(), calls=%async_computation.3 | async-start | bytes 2121728
  17.6 18.0 %copy-start.3 = (f32[728]{0:T(1024)S(1)}, f32[728]{0:T(1024)}, u32[]{:S(2)}) copy-start(f32[728]{0:T(1024)} %param.11) | copy-start | bytes 8740
  36.8 3.6 %copy-start.5 = (u32[32]{0:T(128)S(1)}, u32[32]{0:T(128)}, u32[]{:S(2)}) copy-start(u32[32]{0:T(128)} %constant.29) | copy-start | bytes 388
  36.8 4.8 %copy-start.4 = (u32[32]{0:T(128)S(1)}, u32[32]{0:T(128)}, u32[]{:S(2)}) copy-start(u32[32]{0:T(128)} %constant.23) | copy-start | bytes 388
  40.3 155.7 %all-reduce.9.cloned.1.call-start = ((), (), s32[]{:S(2)}) async-start(), calls=%async_computation.2 | async-start | bytes 8486912
Sparse Core Ops, SparseCore 0:
  40.4 53.0 all-reduce.10
  98.2 97.8 all-reduce.8
